TPU v7x, 32 devices: a whole 2x2x4 slice. The times are simulated.
32 devices in a mesh: tm: 4 (over z), space: 8 (over y, x, core).
Axes of the slice: x: 2, y: 2, z: 4, core: 2. Of those that a mesh axis runs over, the one named last changes fastest.
Arguments:
- queries: bfloat16 [4, 1024, 1120], P('tm', 'space'), may hold values from -6 to 6
- keys_in: bfloat16 [4, 1024, 1120], P('tm', 'space'), may hold values from -30 to 30
- values_in: bfloat16 [4, 1024, 1120], P('tm', 'space'), may hold values from -10 to 10
- grad_attn: bfloat16 [4, 1024, 1120], P('tm', 'space'), may hold values from -6 to 6
Outputs:
- mixed: bfloat16 [4, 1024, 1120], P('tm', 'space')
- grad_queries: bfloat16 [4, 1024, 1120], P('tm', 'space')
- grad_keys: bfloat16 [4, 1024, 1120], P('tm', 'space')
- values_gradient: bfloat16 [4, 1024, 1120], P('tm', 'space')
All inputs are finite; a program needn't handle non-finite values.
Results may differ from a plain program's by a relative error of at most 0.001.
Values sent between devices are 32-bit elements; how exact they have to be, the bound alone decides.
A program may use at most 64 MiB of HBM per device.

v0:
```python
import jax
import jax.numpy as jnp
from jax import lax
from jax.sharding import PartitionSpec as P

HEAD_DIM = 112


HIGH_PRECISION = lax.Precision.HIGHEST


def prefix(value, axis, join, neutral, backward):
    count, mine = (lax.axis_size(axis), lax.axis_index(axis))
    pieces = jax.tree.map(lambda part: lax.all_gather(part, axis), value)
    if backward:
        pieces = jax.tree.map(lambda part: part[::-1], pieces)
        mine = count - 1 - mine
    subtotal = jax.tree.map(
        lambda part, zero: jnp.full_like(part, 0) + jnp.asarray(zero, part.dtype), value, neutral
    )

    def hop(position, subtotal):
        longer = join(subtotal, jax.tree.map(lambda part: part[position], pieces))
        return jax.tree.map(lambda new, old: jnp.where(position < mine, new, old), longer, subtotal)

    return lax.fori_loop(0, count - 1, hop, subtotal)


def add_pair(earlier, later):
    return (earlier[0] + later[0], earlier[1] + later[1])


def running_states(local_state, local_total):
    shares = (
        lax.psum_scatter(local_state, "space", scatter_dimension=0, tiled=True),
        lax.psum_scatter(local_total, "space", scatter_dimension=0, tiled=True),
    )
    before = prefix(
        (shares[0], shares[1]),
        "tm",
        add_pair,
        (jnp.zeros_like(shares[0]), jnp.zeros_like(shares[1])),
        False,
    )
    running = add_pair(before, shares)
    return (
        lax.all_gather(running[0], "space", axis=0, tiled=True),
        lax.all_gather(running[1], "space", axis=0, tiled=True),
    )


def later_states(local_state, local_total):
    shares = (
        lax.psum_scatter(local_state, "space", scatter_dimension=0, tiled=True),
        lax.psum_scatter(local_total, "space", scatter_dimension=0, tiled=True),
    )
    after = prefix(
        (shares[0], shares[1]),
        "tm",
        add_pair,
        (jnp.zeros_like(shares[0]), jnp.zeros_like(shares[1])),
        True,
    )
    running = add_pair(after, shares)
    return (
        lax.all_gather(running[0], "space", axis=0, tiled=True),
        lax.all_gather(running[1], "space", axis=0, tiled=True),
    )


def body(queries, keys_in, values_in, grad_attn):
    row_count = queries.shape[1]
    channels = queries.shape[2]
    heads = channels // HEAD_DIM
    query_rows = queries[0]
    key_rows = keys_in[0]
    value_rows = values_in[0]
    key_pos = jax.nn.relu(key_rows)
    state_part = jnp.einsum(
        "isp,isz->spz",
        key_pos.reshape(row_count, heads, HEAD_DIM),
        value_rows.reshape(row_count, heads, HEAD_DIM),
        preferred_element_type=jnp.float32,
    )
    total_part = jnp.sum(key_pos, axis=0, dtype=jnp.float32)
    state_flat, total_flat = running_states(state_part.reshape(channels, HEAD_DIM), total_part)
    running_state = state_flat.reshape(heads, HEAD_DIM, HEAD_DIM)
    running_total = total_flat.reshape(heads, HEAD_DIM)
    query_position = jax.nn.relu(query_rows).astype(jnp.float32).reshape(row_count, heads, HEAD_DIM)
    numerator = jnp.einsum("igx,gxb->igb", query_position, running_state, precision=HIGH_PRECISION)
    denom = jnp.einsum("rhk,hk->rh", query_position, running_total, precision=HIGH_PRECISION) + 1.0
    attn_f = numerator / denom[..., None]
    mixed = attn_f.reshape(row_count, channels).astype(jnp.bfloat16)
    g_out = grad_attn[0].astype(jnp.float32).reshape(row_count, heads, HEAD_DIM)
    numerator_gradient = g_out / denom[..., None]
    denominator_gradient = -jnp.sum(g_out * attn_f, axis=-1) / denom
    feature_gradient = (
        jnp.einsum("tqd,qwd->tqw", numerator_gradient, running_state, precision=HIGH_PRECISION)
        + denominator_gradient[..., None] * running_total[None]
    )
    grad_queries = jnp.where(
        query_rows.reshape(row_count, heads, HEAD_DIM) > 0, feature_gradient, 0.0
    )
    partial_state_gradient = jnp.einsum(
        "isp,isz->spz", query_position, numerator_gradient, precision=HIGH_PRECISION
    )
    gtotal_part = jnp.einsum(
        "rhk,rh->hk", query_position, denominator_gradient, precision=HIGH_PRECISION
    )
    gstate_flat, gtotal_flat = later_states(
        partial_state_gradient.reshape(channels, HEAD_DIM), gtotal_part.reshape(channels)
    )
    state_gradient = gstate_flat.reshape(heads, HEAD_DIM, HEAD_DIM)
    total_gradient = gtotal_flat.reshape(heads, HEAD_DIM)
    key_wide_float = key_pos.astype(jnp.float32).reshape(row_count, heads, HEAD_DIM)
    value_wide_float = value_rows.astype(jnp.float32).reshape(row_count, heads, HEAD_DIM)
    values_gradient = jnp.einsum(
        "igx,gxb->igb", key_wide_float, state_gradient, precision=HIGH_PRECISION
    )
    key_gradient = (
        jnp.einsum("tqd,qwd->tqw", value_wide_float, state_gradient, precision=HIGH_PRECISION)
        + total_gradient[None]
    )
    grad_keys = jnp.where(key_rows.reshape(row_count, heads, HEAD_DIM) > 0, key_gradient, 0.0)
    return (
        mixed[None],
        grad_queries.reshape(row_count, channels).astype(jnp.bfloat16)[None],
        grad_keys.reshape(row_count, channels).astype(jnp.bfloat16)[None],
        values_gradient.reshape(row_count, channels).astype(jnp.bfloat16)[None],
    )


def solution(mesh):
    placed = (
        P("tm", "space", None),
        P("tm", "space", None),
        P("tm", "space", None),
        P("tm", "space", None),
    )
    return jax.shard_map(
        body,
        mesh=mesh,
        in_specs=placed,
        out_specs=(
            P("tm", "space", None),
            P("tm", "space", None),
            P("tm", "space", None),
            P("tm", "space", None),
        ),
        check_vma=False,
    )
```

profile of v0, /device:TPU:0, one launch (start us, length us, event | category | flops | bytes accessed | tf_op | source)
XLA Modules:
  0.0 177.9 jit_solution(11085069371116808185)
XLA Ops:
  0.6 0.0 copy-start
  0.6 1.0 broadcast_maximum_fusion.1
  1.7 0.0 copy-done
  1.7 0.3 fusion.17
  2.0 0.0 copy-start.1
  2.0 19.4 %fusion = f32[144,112]{1,0:T(8,128)S(1)} fusion(f32[1120,112]{1,0:T(8,128)S(1)} %bitcast.97), kind=kCustom, calls=%all-reduce-scatter | all-reduce-scatter fusion | flops 129025 | bytes 566784
  21.4 1.3 collective-permute-start
  22.7 0.0 copy-done.1
  22.7 0.2 convert_reduce_fusion
  22.9 0.0 copy-start.2
  22.9 0.1 broadcast_compare_fusion
  23.0 0.9 copy-done.2
  23.9 0.1 broadcast_compare_fusion.1
  24.0 12.3 %all-reduce.5 = f32[1120]{0:T(1024)S(1)} all-reduce(f32[1120]{0:T(1024)S(1)} %convert_reduce_fusion), channel_id=7, replica_groups=mesh['tm'=4,'space'=8] {'space'}, use_global_device_ids=true, to_apply=%region_2.3.clone | all-reduce | flops 1120 | bytes 8960
  36.3 0.0 copy-start.5
  36.4 0.6 copy-done.5
  37.0 0.0 copy-start.3
  37.0 0.6 dynamic-slice
  37.6 0.1 copy-done.3
  37.7 0.6 fusion.16
  39.6 0.2 dynamic-slice_dynamic-update-slice_fusion.1
  40.4 11.9 %all-reduce = f32[560]{0:T(1024)S(1)} all-reduce(f32[560]{0:T(1024)S(1)} %dynamic-slice_dynamic-update-slice_fusion.1), channel_id=3, replica_groups=mesh['tm'=4,'space'=8] {'tm'}, use_global_device_ids=true, to_apply=%add | all-reduce | flops 560 | bytes 4480
  52.3 0.1 reshape.108
  53.1 0.0 collective-permute-done
  53.1 0.3 concatenate
  53.4 13.9 %all-gather.4 = f32[4,140,112]{2,1,0:T(8,128)S(1)} all-gather(f32[1,140,112]{2,1,0:T(8,128)S(1)} %dynamic-slice_bitcast_fusion.1), channel_id=2, replica_groups=mesh['tm'=4,'space'=8] {'tm'}, dimensions={0}, use_global_device_ids=true | all-gather | bytes 313600 | tf_op jit(solution)/shard_map/all_gather | solution.py:14
  67.3 0.2 while.32
  67.5 0.2 add_dynamic-update-slice_fusion.1
  67.7 12.0 %all-reduce.1 = f32[1120]{0:T(1024)S(1)} all-reduce(f32[1120]{0:T(1024)S(1)} %add_dynamic-update-slice_fusion.1), channel_id=1, replica_groups=mesh['tm'=4,'space'=8] {'space'}, use_global_device_ids=true, to_apply=%add.1 | all-reduce | flops 1120 | bytes 8960
  79.8 0.1 reshape.149
  79.9 0.1 reshape.102
  80.0 0.3 fusion.18
  80.3 12.8 %all-gather.5 = f32[8,140,112]{2,1,0:T(8,128)S(1)} all-gather(f32[1,140,112]{2,1,0:T(8,128)S(1)} %add_bitcast_fusion.1), channel_id=1, replica_groups=mesh['tm'=4,'space'=8] {'space'}, dimensions={0}, use_global_device_ids=true | all-gather | bytes 564480 | tf_op jit(solution)/shard_map/all_gather | solution.py:47
  93.1 0.0 copy-start.4
  93.2 0.9 copy-done.4
  94.1 0.7 fusion.10
  94.8 1.4 fusion.9
  96.2 0.5 fusion.14
  96.7 0.1 reshape.104
  96.8 13.5 %all-reduce.7 = f32[1120]{0:T(1024)S(1)} all-reduce(f32[1120]{0:T(1024)S(1)} %reshape.104), channel_id=9, replica_groups=mesh['tm'=4,'space'=8] {'space'}, use_global_device_ids=true, to_apply=%region_7.8.clone | all-reduce | flops 1120 | bytes 8960
  110.3 15.7 %fusion.1 = f32[144,112]{1,0:T(8,128)S(1)} fusion(f32[1120,112]{1,0:T(8,128)S(1)} %bitcast.99), kind=kCustom, calls=%all-reduce-scatter.1 | all-reduce-scatter fusion | flops 129025 | bytes 566784
  126.0 1.3 collective-permute-start.1
  127.3 1.5 fusion.8
  128.8 0.2 dynamic-slice_dynamic-update-slice_fusion
  129.0 8.7 %all-reduce.2 = f32[560]{0:T(1024)S(1)} all-reduce(f32[560]{0:T(1024)S(1)} %dynamic-slice_dynamic-update-slice_fusion), channel_id=5, replica_groups=mesh['tm'=4,'space'=8] {'tm'}, use_global_device_ids=true, to_apply=%add.2 | all-reduce | flops 560 | bytes 4480
  137.7 0.1 reshape.110
  137.8 0.1 rev.7
  137.9 0.0 collective-permute-done.1
  137.9 0.3 concatenate.1
  138.2 14.7 %all-gather.6 = f32[4,140,112]{2,1,0:T(8,128)S(1)} all-gather(f32[1,140,112]{2,1,0:T(8,128)S(1)} %dynamic-slice_bitcast_fusion), channel_id=4, replica_groups=mesh['tm'=4,'space'=8] {'tm'}, dimensions={0}, use_global_device_ids=true | all-gather | bytes 313600 | tf_op jit(solution)/shard_map/all_gather | solution.py:14
  152.9 0.2 while.33
  153.2 0.2 add_dynamic-update-slice_fusion
  153.4 12.0 %all-reduce.3 = f32[1120]{0:T(1024)S(1)} all-reduce(f32[1120]{0:T(1024)S(1)} %add_dynamic-update-slice_fusion), channel_id=1, replica_groups=mesh['tm'=4,'space'=8] {'space'}, use_global_device_ids=true, to_apply=%add.3 | all-reduce | flops 1120 | bytes 8960
  165.4 0.1 add.125
  165.5 9.8 %all-gather.7 = f32[8,140,112]{2,1,0:T(8,128)S(1)} all-gather(f32[1,140,112]{2,1,0:T(8,128)S(1)} %add_bitcast_fusion), channel_id=1, replica_groups=mesh['tm'=4,'space'=8] {'space'}, dimensions={0}, use_global_device_ids=true | all-gather | bytes 564480 | tf_op jit(solution)/shard_map/all_gather | solution.py:66
  175.4 1.3 convolution_convert_fusion
  176.7 1.2 fusion.7
  (39 shorter events, 0.4 us)
Async XLA Ops:
  0.6 1.1 copy-start
  2.0 20.7 %copy-start.1 = (bf16[1,128,1120]{1,2,0:T(8,128)(2,1)S(1)}, bf16[1,128,1120]{1,2,0:T(8,128)(2,1)}, u32[]{:S(2)}) copy-start(bf16[1,128,1120]{1,2,0:T(8,128)(2,1)} %param.9) | copy-start | bytes 860164
  21.4 31.7 %collective-permute-start = (f32[28,112]{1,0:T(8,128)S(1)}, f32[28,112]{1,0:T(8,128)S(1)}, u32[]{:S(2)}, u32[]{:S(2)}) collective-permute-start(f32[28,112]{1,0:T(8,128)S(1)} %slice), channel_id=1, source_target_pairs={{0,1},{1,2},{2,3},{3,4},{4,5},{5,6},{6,7},{8,9},{9,10},{10,11},{11... | collective-permute-start | bytes 37640
  22.9 1.0 copy-start.2
  36.3 0.7 copy-start.5
  37.0 0.7 copy-start.3
  93.1 1.0 copy-start.4
  126.0 11.8 %collective-permute-start.1 = (f32[28,112]{1,0:T(8,128)S(1)}, f32[28,112]{1,0:T(8,128)S(1)}, u32[]{:S(2)}, u32[]{:S(2)}) collective-permute-start(f32[28,112]{1,0:T(8,128)S(1)} %slice.1), channel_id=1, source_target_pairs={{0,1},{1,2},{2,3},{3,4},{4,5},{5,6},{6,7},{8,9},{9,10},{10,11},{11... | collective-permute-start | bytes 37640
where the time goes:
time: 178 us
  blocking collectives  157 us (88%)
  matrix products  7.28 us (4%)
  local copies, waits for them, and re-layouts  5.37 us (3%)
  between operations  3.56 us (2%)
  starting transfers between devices  2.58 us (1%)
  other arithmetic  1.99 us (1%)
    unnamed x8, blocking collectives  106 us
    all_gather x2, blocking collectives, prefix(): pieces = jax.tree.map(lambda part: lax.all_gather(part, axis), value)  28.6 us
    all_gather x1, blocking collectives, running_states(): lax.all_gather(running[0], 'space', axis=0, tiled=True)  12.8 us
    all_gather x1, blocking collectives, later_states(): lax.all_gather(running[0], 'space', axis=0, tiled=True)  9.84 us
    unnamed x26, local copies, waits for them, and re-layouts  4.69 us
  transfers between devices with their start and end apart: 2, of which 0 were waited for; matrix products, arithmetic and copies ran while one was open for 2% of the time, Pallas kernels for 0%

commit v1 on v0

v1 whole, which is shorter than its diff:
```python
import functools

import jax
import jax.numpy as jnp
from jax import lax
from jax.experimental import pallas as pl
from jax.experimental.pallas import tpu as pltpu
from jax.sharding import PartitionSpec as P

HEAD_DIM = 112
LANES = 128
SUBLANES = 8
CHUNKS = 2
MESH = pl.DeviceIdType.MESH


def split_heads(heads):
    count = min(CHUNKS, heads)
    base, extra = divmod(heads, count)
    chunks, first = [], 0
    for index in range(count):
        size = base + (1 if index < extra else 0)
        chunks.append((first, size))
        first += size
    return chunks


def two_terms(value):
    high = value.astype(jnp.bfloat16)
    low = (value - high.astype(jnp.float32)).astype(jnp.bfloat16)
    return high, low


def nn(a, b):
    return lax.dot_general(a, b, (((1,), (0,)), ((), ())), preferred_element_type=jnp.float32)


def nt(a, b):
    return lax.dot_general(a, b, (((1,), (1,)), ((), ())), preferred_element_type=jnp.float32)


def tn(a, b):
    return lax.dot_general(a, b, (((0,), (0,)), ((), ())), preferred_element_type=jnp.float32)


def kernel(
    n_space, n_tm, chunks, piece,
    q_ref, k_ref, v_ref, g_ref,
    mixed_ref, gq_ref, gk_ref, gv_ref,
    local, incoming, reduced, earlier, running, whole,
    rs_send, rs_recv, tm_send, tm_recv, ag_send, ag_recv,
):
    me = lax.axis_index("space")
    group = lax.axis_index("tm")
    rows = q_ref.shape[1]
    spare = LANES - HEAD_DIM
    columns = lax.broadcasted_iota(jnp.int32, (rows, spare), 1)

    barrier = pltpu.get_barrier_semaphore()
    for d in range(1, n_space):
        pl.semaphore_signal(
            barrier, inc=1, device_id={"space": lax.rem(me + d, n_space)}, device_id_type=MESH
        )
    for d in range(1, n_tm):
        pl.semaphore_signal(
            barrier, inc=1, device_id={"tm": lax.rem(group + d, n_tm)}, device_id_type=MESH
        )

    def head(ref, h):
        return ref[0, :, h * HEAD_DIM:(h + 1) * HEAD_DIM]

    def value_wide(h, ones):
        tail = jnp.where(columns < ones, 1.0, 0.0).astype(jnp.bfloat16)
        return jnp.concatenate([head(v_ref, h), tail], axis=1)

    def scatter_copy(phase, c, d):
        peer = lax.rem(me + d, n_space)
        return pltpu.make_async_remote_copy(
            src_ref=local.at[phase, c, pl.ds(pl.multiple_of(peer * piece, SUBLANES), piece)],
            dst_ref=incoming.at[phase, c, d - 1],
            send_sem=rs_send.at[phase, c, d - 1],
            recv_sem=rs_recv.at[phase, c, d - 1],
            device_id={"space": peer},
            device_id_type=MESH,
        )

    def group_copy(phase, c, d):
        peer = group + d if phase == 0 else group - d
        peer = jnp.clip(peer, 0, n_tm - 1)
        return pltpu.make_async_remote_copy(
            src_ref=reduced.at[phase, c],
            dst_ref=earlier.at[phase, c, d - 1],
            send_sem=tm_send.at[phase, c, d - 1],
            recv_sem=tm_recv.at[phase, c, d - 1],
            device_id={"tm": peer},
            device_id_type=MESH,
        )

    def gather_copy(phase, c, d):
        peer = lax.rem(me + d, n_space)
        return pltpu.make_async_remote_copy(
            src_ref=running.at[phase, c],
            dst_ref=whole.at[phase, c, pl.ds(pl.multiple_of(me * piece, SUBLANES), piece)],
            send_sem=ag_send.at[phase, c, d - 1],
            recv_sem=ag_recv.at[phase, c, d - 1],
            device_id={"space": peer},
            device_id_type=MESH,
        )

    def sends_to(phase, d):
        return group + d < n_tm if phase == 0 else group - d >= 0

    def hears_from(phase, d):
        return group - d >= 0 if phase == 0 else group + d < n_tm

    def scatter(phase, c):
        for d in range(1, n_space):
            scatter_copy(phase, c, d).start()

    def reduce(phase, c):
        total = local[phase, c, pl.ds(pl.multiple_of(me * piece, SUBLANES), piece)]
        for d in range(1, n_space):
            scatter_copy(phase, c, d).wait_recv()
            total = total + incoming[phase, c, d - 1]
        reduced[phase, c] = total
        running[phase, c] = total
        for d in range(1, n_tm):
            @pl.when(sends_to(phase, d))
            def _():
                group_copy(phase, c, d).start()

    def gather(phase, c):
        for d in range(1, n_tm):
            @pl.when(hears_from(phase, d))
            def _():
                group_copy(phase, c, d).wait_recv()
                running[phase, c] = running[phase, c] + earlier[phase, c, d - 1]
        for d in range(1, n_space):
            gather_copy(phase, c, d).start()
        whole[phase, c, pl.ds(pl.multiple_of(me * piece, SUBLANES), piece)] = running[phase, c]

    def arrive(phase, c):
        for d in range(1, n_space):
            gather_copy(phase, c, d).wait_recv()

    def pad(phase, c, size):
        spare_rows = n_space * piece - size * HEAD_DIM
        if spare_rows:
            local[phase, c, pl.ds(size * HEAD_DIM, spare_rows)] = jnp.zeros(
                (spare_rows, LANES), jnp.float32
            )

    def states(c):
        first, size = chunks[c]
        for i in range(size):
            h = first + i
            key_pos = jnp.maximum(head(k_ref, h), 0)
            local[0, c, pl.ds(i * HEAD_DIM, HEAD_DIM)] = tn(key_pos, value_wide(h, 2))
        pad(0, c, size)

    def queries(c):
        first, size = chunks[c]
        for i in range(size):
            h = first + i
            high, low = two_terms(whole[0, c, pl.ds(i * HEAD_DIM, HEAD_DIM)])
            query = head(q_ref, h)
            query_pos = jnp.maximum(query, 0)
            numer = nn(query_pos, high) + nn(query_pos, low)
            inverse = 1.0 / (numer[:, HEAD_DIM:HEAD_DIM + 1] + 1.0)
            attn = numer[:, :HEAD_DIM] * inverse
            mixed_ref[0, :, h * HEAD_DIM:(h + 1) * HEAD_DIM] = attn.astype(jnp.bfloat16)
            g_out = head(g_ref, h)
            g_wide = g_out.astype(jnp.float32)
            against = -jnp.sum(g_wide * attn, axis=1, keepdims=True)
            against_high, against_low = two_terms(against)
            tail = jnp.where(
                columns == 0,
                against_high.astype(jnp.float32),
                jnp.where(columns == 1, against_low.astype(jnp.float32), 0.0),
            ).astype(jnp.bfloat16)
            left = jnp.concatenate([g_out, tail], axis=1)
            feature = (nt(left, high) + nt(left, low)) * inverse
            gq_ref[0, :, h * HEAD_DIM:(h + 1) * HEAD_DIM] = jnp.where(
                query.astype(jnp.float32) > 0, feature, 0.0
            ).astype(jnp.bfloat16)
            right = jnp.concatenate(
                [g_wide, jnp.where(columns == 0, against, 0.0)], axis=1
            ) * inverse
            right_high, right_low = two_terms(right)
            local[1, c, pl.ds(i * HEAD_DIM, HEAD_DIM)] = tn(query_pos, right_high) + tn(
                query_pos, right_low
            )
        pad(1, c, size)

    def keys(c):
        first, size = chunks[c]
        for i in range(size):
            h = first + i
            high, low = two_terms(whole[1, c, pl.ds(i * HEAD_DIM, HEAD_DIM)])
            key = head(k_ref, h)
            key_pos = jnp.maximum(key, 0)
            value_gradient = nn(key_pos, high) + nn(key_pos, low)
            gv_ref[0, :, h * HEAD_DIM:(h + 1) * HEAD_DIM] = value_gradient[:, :HEAD_DIM].astype(
                jnp.bfloat16
            )
            value = value_wide(h, 1)
            key_gradient = nt(value, high) + nt(value, low)
            gk_ref[0, :, h * HEAD_DIM:(h + 1) * HEAD_DIM] = jnp.where(
                key.astype(jnp.float32) > 0, key_gradient, 0.0
            ).astype(jnp.bfloat16)

    count = len(chunks)
    for c in range(count):
        states(c)
        if c == 0:
            pl.semaphore_wait(barrier, n_space - 1 + n_tm - 1)
        scatter(0, c)
    for c in range(count):
        reduce(0, c)
    for c in range(count):
        gather(0, c)
    for c in range(count):
        arrive(0, c)
        queries(c)
        scatter(1, c)
    for c in range(count):
        reduce(1, c)
    for c in range(count):
        gather(1, c)
    for c in range(count):
        arrive(1, c)
        keys(c)
    for phase in range(2):
        for c in range(count):
            for d in range(1, n_space):
                scatter_copy(phase, c, d).wait_send()
                gather_copy(phase, c, d).wait_send()
            for d in range(1, n_tm):
                @pl.when(sends_to(phase, d))
                def _():
                    group_copy(phase, c, d).wait_send()


def solution(mesh):
    n_space, n_tm = mesh.shape["space"], mesh.shape["tm"]
    spec = P("tm", "space", None)

    def body(queries, keys_in, values_in, grad_attn):
        heads = queries.shape[2] // HEAD_DIM
        chunks = split_heads(heads)
        largest = max(size for _, size in chunks)
        piece = -(-largest * HEAD_DIM // (SUBLANES * n_space)) * SUBLANES
        count = len(chunks)
        vmem = pl.BlockSpec(memory_space=pltpu.VMEM)
        f32 = jnp.float32
        dma = pltpu.SemaphoreType.DMA
        peers, others = max(n_space - 1, 1), max(n_tm - 1, 1)
        return pl.pallas_call(
            functools.partial(kernel, n_space, n_tm, chunks, piece),
            out_shape=[jax.ShapeDtypeStruct(queries.shape, jnp.bfloat16)] * 4,
            in_specs=[vmem] * 4,
            out_specs=[vmem] * 4,
            scratch_shapes=[
                pltpu.VMEM((2, count, n_space * piece, LANES), f32),
                pltpu.VMEM((2, count, peers, piece, LANES), f32),
                pltpu.VMEM((2, count, piece, LANES), f32),
                pltpu.VMEM((2, count, others, piece, LANES), f32),
                pltpu.VMEM((2, count, piece, LANES), f32),
                pltpu.VMEM((2, count, n_space * piece, LANES), f32),
                dma((2, count, peers)),
                dma((2, count, peers)),
                dma((2, count, others)),
                dma((2, count, others)),
                dma((2, count, peers)),
                dma((2, count, peers)),
            ],
            compiler_params=pltpu.CompilerParams(collective_id=0, has_side_effects=True),
        )(queries, keys_in, values_in, grad_attn)

    return jax.shard_map(
        lambda *args: tuple(body(*args)),
        mesh=mesh,
        in_specs=(spec,) * 4,
        out_specs=(spec,) * 4,
        check_vma=False,
    )
```

time: 178 us -> 57.7 us (0.32)
  blocking collectives: 157 us -> 0 us
  Pallas kernels: 0 us -> 47.4 us
  matrix products: 7.28 us -> 0 us
  local copies, waits for them, and re-layouts: 5.37 us -> 9.39 us
  between operations: 3.56 us -> 0.66 us
  starting transfers between devices: 2.58 us -> 0 us
  other arithmetic: 1.99 us -> 0 us
    unnamed x8 -> x0, blocking collectives: 106 us -> none
    all_gather x4 -> x0, blocking collectives: 51.3 us -> none  [the longest x2 28.6 us: prefix(): pieces = jax.tree.map(lambda part: lax.all_gather(part, axis), value)]
    pallas_call x0 -> x1, Pallas kernels: none -> 47.4 us  [body(): pl.pallas_call(functools.partial(kernel, n_space, n_tm, chunks, piece), o...]
    dot_general x8 -> x0, matrix products: 7.28 us -> none  [the longest x1 1.52 us: body(): jnp.einsum('tqd,qwd->tqw', numerator_gradient, running_state, precision=H...]
    pallas_call x0 -> x4, local copies, waits for them, and re-layouts: none -> 4.52 us  [body(): pl.pallas_call(functools.partial(kernel, n_space, n_tm, chunks, piece), o...]
    unnamed x2 -> x0, starting transfers between devices: 2.58 us -> none
    unnamed x26 -> x16, local copies, waits for them, and re-layouts: 4.69 us -> 4.87 us
  transfers between devices with their start and end apart: 2 -> 0, of which waited for: 0 -> 0; matrix products, arithmetic and copies ran while one was open for 2% -> 0% of each run, Pallas kernels for 0% -> 0%
where the time goes in v1:
time: 57.7 us; the launch traced here: 57.4 us
  Pallas kernels  47.4 us (82%)
  local copies, waits for them, and re-layouts  9.39 us (16%)
  between operations  0.66 us (1%)
    pallas_call x1, Pallas kernels, body(): pl.pallas_call(functools.partial(kernel, n_space, n_tm, chunks, piece), o...  47.4 us
    unnamed x16, local copies, waits for them, and re-layouts  4.87 us
    pallas_call x4, local copies, waits for them, and re-layouts, body(): pl.pallas_call(functools.partial(kernel, n_space, n_tm, chunks, piece), o...  4.52 us

profile of v1, /device:TPU:0, one launch (start us, length us, event | category | flops | bytes accessed | tf_op | source)
XLA Modules:
  0.0 57.4 jit_solution(12135043810610476923)
XLA Ops:
  0.6 0.0 copy-start.3
  0.6 1.9 %copy.8.q_ref = bf16[1,128,1120]{2,1,0:T(8,128)(2,1)} copy(bf16[1,128,1120]{1,2,0:T(8,128)(2,1)} %param.4) | data formatting | bytes 573440 | tf_op args[0]
  2.5 0.0 copy-done.3
  2.5 0.0 copy-start.4
  2.5 0.9 %copy.9.k_ref = bf16[1,128,1120]{2,1,0:T(8,128)(2,1)} copy(bf16[1,128,1120]{1,2,0:T(8,128)(2,1)S(1)} %copy-done.3) | data formatting | bytes 573440 | tf_op args[1]
  3.4 0.1 copy-done.4
  3.5 0.0 copy-start.5
  3.5 0.9 %copy.10.v_ref = bf16[1,128,1120]{2,1,0:T(8,128)(2,1)} copy(bf16[1,128,1120]{1,2,0:T(8,128)(2,1)S(1)} %copy-done.4) | data formatting | bytes 573440 | tf_op args[2]
  4.4 0.1 copy-done.5
  4.4 0.9 %copy.11.g_ref = bf16[1,128,1120]{2,1,0:T(8,128)(2,1)} copy(bf16[1,128,1120]{1,2,0:T(8,128)(2,1)S(1)} %copy-done.5) | data formatting | bytes 573440 | tf_op args[3]
  5.3 47.4 %shard_map.75 = (bf16[1,128,1120]{2,1,0:T(8,128)(2,1)}, bf16[1,128,1120]{2,1,0:T(8,128)(2,1)}, bf16[1,128,1120]{2,1,0:T(8,128)(2,1)}, bf16[1,128,1120]{2,1,0:T(8,128)(2,1)}) custom-call(bf16[1,128,1120]{2,1,0:T(8,128)(2,1)} %copy.8.q_ref, bf16[1,128,1120]{2,1,0:T(8,128)(2,1)} %copy.9.k_ref, bf16[1,128,1120]{2,1,0:T(8,128)(2,1)} %copy.10.v_ref, ...), custom_call_target="tpu_custom_call" | custom-call | tf_op jit(solution)/shard_map/pallas_call | solution.py:258
  52.7 0.0 copy-start.2
  52.7 1.9 %copy.12 = bf16[1,128,1120]{1,2,0:T(8,128)(2,1)} copy(bf16[1,128,1120]{2,1,0:T(8,128)(2,1)} %get-tuple-element.4) | data formatting | bytes 573440 | tf_op jit(solution)/shard_map/pallas_call | solution.py:258
  54.6 0.0 copy-done.2
  54.6 0.0 copy-start.1
  54.6 0.9 %copy.13 = bf16[1,128,1120]{1,2,0:T(8,128)(2,1)} copy(bf16[1,128,1120]{2,1,0:T(8,128)(2,1)S(1)} %copy-done.2) | data formatting | bytes 573440 | tf_op jit(solution)/shard_map/pallas_call | solution.py:258
  55.5 0.1 copy-done.1
  55.6 0.0 copy-start
  55.6 0.9 %copy.14 = bf16[1,128,1120]{1,2,0:T(8,128)(2,1)} copy(bf16[1,128,1120]{2,1,0:T(8,128)(2,1)S(1)} %copy-done.1) | data formatting | bytes 573440 | tf_op jit(solution)/shard_map/pallas_call | solution.py:258
  56.5 0.1 copy-done
  56.5 0.9 %copy.15 = bf16[1,128,1120]{1,2,0:T(8,128)(2,1)} copy(bf16[1,128,1120]{2,1,0:T(8,128)(2,1)S(1)} %copy-done) | data formatting | bytes 573440 | tf_op jit(solution)/shard_map/pallas_call | solution.py:258
Async XLA Ops:
  0.6 1.9 %copy-start.3 = (bf16[1,128,1120]{1,2,0:T(8,128)(2,1)S(1)}, bf16[1,128,1120]{1,2,0:T(8,128)(2,1)}, u32[]{:S(2)}) copy-start(bf16[1,128,1120]{1,2,0:T(8,128)(2,1)} %param.5) | copy-start | bytes 860164
  2.5 1.0 %copy-start.4 = (bf16[1,128,1120]{1,2,0:T(8,128)(2,1)S(1)}, bf16[1,128,1120]{1,2,0:T(8,128)(2,1)}, u32[]{:S(2)}) copy-start(bf16[1,128,1120]{1,2,0:T(8,128)(2,1)} %param.6) | copy-start | bytes 860164
  3.5 1.0 %copy-start.5 = (bf16[1,128,1120]{1,2,0:T(8,128)(2,1)S(1)}, bf16[1,128,1120]{1,2,0:T(8,128)(2,1)}, u32[]{:S(2)}) copy-start(bf16[1,128,1120]{1,2,0:T(8,128)(2,1)} %param.7) | copy-start | bytes 860164
  52.7 1.9 %copy-start.2 = (bf16[1,128,1120]{2,1,0:T(8,128)(2,1)S(1)}, bf16[1,128,1120]{2,1,0:T(8,128)(2,1)}, u32[]{:S(2)}) copy-start(bf16[1,128,1120]{2,1,0:T(8,128)(2,1)} %get-tuple-element.5) | copy-start | bytes 860164
  54.6 1.0 %copy-start.1 = (bf16[1,128,1120]{2,1,0:T(8,128)(2,1)S(1)}, bf16[1,128,1120]{2,1,0:T(8,128)(2,1)}, u32[]{:S(2)}) copy-start(bf16[1,128,1120]{2,1,0:T(8,128)(2,1)} %get-tuple-element.6) | copy-start | bytes 860164
  55.6 1.0 %copy-start = (bf16[1,128,1120]{2,1,0:T(8,128)(2,1)S(1)}, bf16[1,128,1120]{2,1,0:T(8,128)(2,1)}, u32[]{:S(2)}) copy-start(bf16[1,128,1120]{2,1,0:T(8,128)(2,1)} %get-tuple-element.7) | copy-start | bytes 860164

commit v2 on v1

--- a/solution.py
+++ b/solution.py
@@ -52,9 +52,9 @@
 ):
     me = lax.axis_index("space")
     group = lax.axis_index("tm")
-    rows = q_ref.shape[1]
+    rows = q_ref.shape[2]
     spare = LANES - HEAD_DIM
-    columns = lax.broadcasted_iota(jnp.int32, (rows, spare), 1)
+    ids = lax.broadcasted_iota(jnp.int32, (spare, rows), 0)
 
     barrier = pltpu.get_barrier_semaphore()
     for d in range(1, n_space):
@@ -66,12 +66,12 @@
             barrier, inc=1, device_id={"tm": lax.rem(group + d, n_tm)}, device_id_type=MESH
         )
 
-    def head(ref, h):
-        return ref[0, :, h * HEAD_DIM:(h + 1) * HEAD_DIM]
+    def span(h):
+        return pl.ds(h * HEAD_DIM, HEAD_DIM)
 
     def value_wide(h, ones):
-        tail = jnp.where(columns < ones, 1.0, 0.0).astype(jnp.bfloat16)
-        return jnp.concatenate([head(v_ref, h), tail], axis=1)
+        tail = jnp.where(ids < ones, 1.0, 0.0).astype(jnp.bfloat16)
+        return jnp.concatenate([v_ref[0, span(h)], tail], axis=0)
 
     def scatter_copy(phase, c, d):
         peer = lax.rem(me + d, n_space)
@@ -154,41 +154,42 @@
         first, size = chunks[c]
         for i in range(size):
             h = first + i
-            key_pos = jnp.maximum(head(k_ref, h), 0)
-            local[0, c, pl.ds(i * HEAD_DIM, HEAD_DIM)] = tn(key_pos, value_wide(h, 2))
+            key_pos = jnp.maximum(k_ref[0, span(h)], 0)
+            local[0, c, span(i)] = nt(key_pos, value_wide(h, 2))
         pad(0, c, size)
 
     def queries(c):
         first, size = chunks[c]
         for i in range(size):
             h = first + i
-            high, low = two_terms(whole[0, c, pl.ds(i * HEAD_DIM, HEAD_DIM)])
-            query = head(q_ref, h)
+            high, low = two_terms(whole[0, c, span(i)])
+            query = q_ref[0, span(h)]
             query_pos = jnp.maximum(query, 0)
-            numer = nn(query_pos, high) + nn(query_pos, low)
-            inverse = 1.0 / (numer[:, HEAD_DIM:HEAD_DIM + 1] + 1.0)
-            attn = numer[:, :HEAD_DIM] * inverse
-            mixed_ref[0, :, h * HEAD_DIM:(h + 1) * HEAD_DIM] = attn.astype(jnp.bfloat16)
-            g_out = head(g_ref, h)
+            numer = tn(jnp.concatenate([high, low], axis=0), jnp.concatenate([query_pos] * 2, axis=0))
+            inverse = 1.0 / (numer[HEAD_DIM:HEAD_DIM + 1] + 1.0)
+            attn = numer[:HEAD_DIM] * inverse
+            mixed_ref[0, span(h)] = attn.astype(jnp.bfloat16)
+            g_out = g_ref[0, span(h)]
             g_wide = g_out.astype(jnp.float32)
-            against = -jnp.sum(g_wide * attn, axis=1, keepdims=True)
+            against = -jnp.sum(g_wide * attn, axis=0, keepdims=True)
             against_high, against_low = two_terms(against)
             tail = jnp.where(
-                columns == 0,
+                ids == 0,
                 against_high.astype(jnp.float32),
-                jnp.where(columns == 1, against_low.astype(jnp.float32), 0.0),
+                jnp.where(ids == 1, against_low.astype(jnp.float32), 0.0),
             ).astype(jnp.bfloat16)
-            left = jnp.concatenate([g_out, tail], axis=1)
-            feature = (nt(left, high) + nt(left, low)) * inverse
-            gq_ref[0, :, h * HEAD_DIM:(h + 1) * HEAD_DIM] = jnp.where(
+            feature = nn(
+                jnp.concatenate([high, low], axis=1),
+                jnp.concatenate([g_out, tail, g_out, tail], axis=0),
+            ) * inverse
+            gq_ref[0, span(h)] = jnp.where(
                 query.astype(jnp.float32) > 0, feature, 0.0
             ).astype(jnp.bfloat16)
-            right = jnp.concatenate(
-                [g_wide, jnp.where(columns == 0, against, 0.0)], axis=1
-            ) * inverse
+            right = jnp.concatenate([g_wide, jnp.where(ids == 0, against, 0.0)], axis=0) * inverse
             right_high, right_low = two_terms(right)
-            local[1, c, pl.ds(i * HEAD_DIM, HEAD_DIM)] = tn(query_pos, right_high) + tn(
-                query_pos, right_low
+            local[1, c, span(i)] = nt(
+                jnp.concatenate([query_pos] * 2, axis=1),
+                jnp.concatenate([right_high, right_low], axis=1),
             )
         pad(1, c, size)
 
@@ -196,16 +197,18 @@
         first, size = chunks[c]
         for i in range(size):
             h = first + i
-            high, low = two_terms(whole[1, c, pl.ds(i * HEAD_DIM, HEAD_DIM)])
-            key = head(k_ref, h)
+            high, low = two_terms(whole[1, c, span(i)])
+            key = k_ref[0, span(h)]
             key_pos = jnp.maximum(key, 0)
-            value_gradient = nn(key_pos, high) + nn(key_pos, low)
-            gv_ref[0, :, h * HEAD_DIM:(h + 1) * HEAD_DIM] = value_gradient[:, :HEAD_DIM].astype(
-                jnp.bfloat16
-            )
+            value_gradient = tn(
+                jnp.concatenate([high, low], axis=0), jnp.concatenate([key_pos] * 2, axis=0)
+            )
+            gv_ref[0, span(h)] = value_gradient[:HEAD_DIM].astype(jnp.bfloat16)
             value = value_wide(h, 1)
-            key_gradient = nt(value, high) + nt(value, low)
-            gk_ref[0, :, h * HEAD_DIM:(h + 1) * HEAD_DIM] = jnp.where(
+            key_gradient = nn(
+                jnp.concatenate([high, low], axis=1), jnp.concatenate([value, value], axis=0)
+            )
+            gk_ref[0, span(h)] = jnp.where(
                 key.astype(jnp.float32) > 0, key_gradient, 0.0
             ).astype(jnp.bfloat16)
 
@@ -245,8 +248,9 @@
     n_space, n_tm = mesh.shape["space"], mesh.shape["tm"]
     spec = P("tm", "space", None)
 
-    def body(queries, keys_in, values_in, grad_attn):
-        heads = queries.shape[2] // HEAD_DIM
+    def body(*args):
+        args = [jnp.swapaxes(arg, 1, 2) for arg in args]
+        heads = args[0].shape[1] // HEAD_DIM
         chunks = split_heads(heads)
         largest = max(size for _, size in chunks)
         piece = -(-largest * HEAD_DIM // (SUBLANES * n_space)) * SUBLANES
@@ -255,9 +259,9 @@
         f32 = jnp.float32
         dma = pltpu.SemaphoreType.DMA
         peers, others = max(n_space - 1, 1), max(n_tm - 1, 1)
-        return pl.pallas_call(
+        outs = pl.pallas_call(
             functools.partial(kernel, n_space, n_tm, chunks, piece),
-            out_shape=[jax.ShapeDtypeStruct(queries.shape, jnp.bfloat16)] * 4,
+            out_shape=[jax.ShapeDtypeStruct(args[0].shape, jnp.bfloat16)] * 4,
             in_specs=[vmem] * 4,
             out_specs=[vmem] * 4,
             scratch_shapes=[
@@ -275,10 +279,11 @@
                 dma((2, count, peers)),
             ],
             compiler_params=pltpu.CompilerParams(collective_id=0, has_side_effects=True),
-        )(queries, keys_in, values_in, grad_attn)
+        )(*args)
+        return tuple(jnp.swapaxes(out, 1, 2) for out in outs)
 
     return jax.shard_map(
-        lambda *args: tuple(body(*args)),
+        body,
         mesh=mesh,
         in_specs=(spec,) * 4,
         out_specs=(spec,) * 4,

time: 57.7 us -> 51 us (0.88)
  local copies, waits for them, and re-layouts: 9.39 us -> 4.57 us
  Pallas kernels: 47.4 us -> 45.5 us
    pallas_call x4 -> x0, local copies, waits for them, and re-layouts: 4.52 us -> none  [body(): pl.pallas_call(functools.partial(kernel, n_space, n_tm, chunks, piece), o...]
    pallas_call x1, Pallas kernels: 47.4 us -> 45.5 us  [body(): pl.pallas_call(functools.partial(kernel, n_space, n_tm, chunks, piece), o...]
    unnamed x16 -> x10, local copies, waits for them, and re-layouts: 4.87 us -> 4.57 us
where the time goes in v2:
time: 51 us; the launch traced here: 50.7 us
  Pallas kernels  45.5 us (89%)
  local copies, waits for them, and re-layouts  4.57 us (9%)
  between operations  0.65 us (1%)
    pallas_call x1, Pallas kernels, body(): pl.pallas_call(functools.partial(kernel, n_space, n_tm, chunks, piece), o...  45.5 us
    unnamed x10, local copies, waits for them, and re-layouts  4.57 us

profile of v2, /device:TPU:0, one launch (start us, length us, event | category | flops | bytes accessed | tf_op | source)
XLA Modules:
  0.0 50.7 jit_solution(6930325981672577266)
XLA Ops:
  0.6 45.5 %shard_map.75 = (bf16[1,1120,128]{2,1,0:T(8,128)(2,1)}, bf16[1,1120,128]{2,1,0:T(8,128)(2,1)}, bf16[1,1120,128]{2,1,0:T(8,128)(2,1)}, bf16[1,1120,128]{2,1,0:T(8,128)(2,1)}) custom-call(bf16[1,1120,128]{2,1,0:T(8,128)(2,1)} %bitcast.8, bf16[1,1120,128]{2,1,0:T(8,128)(2,1)} %bitcast.9, bf16[1,1120,128]{2,1,0:T(8,128)(2,1)} %bitcast.10, ...), custom_call_target="tpu_custom_call" | custom-call | tf_op jit(solution)/shard_map/pallas_call | solution.py:262
  46.1 0.0 copy-start.2
  46.2 1.7 %copy.12 = bf16[1,128,1120]{1,2,0:T(8,128)(2,1)} copy(bf16[1,128,1120]{1,2,0:T(8,128)(2,1)} %bitcast.15) | data formatting | bytes 573440
  47.9 0.0 copy-done.2
  47.9 0.0 copy-start.1
  47.9 0.7 %copy.13 = bf16[1,128,1120]{1,2,0:T(8,128)(2,1)} copy(bf16[1,128,1120]{1,2,0:T(8,128)(2,1)S(1)} %bitcast.14) | data formatting | bytes 573440
  48.6 0.3 copy-done.1
  48.9 0.0 copy-start
  49.0 0.7 %copy.14 = bf16[1,128,1120]{1,2,0:T(8,128)(2,1)} copy(bf16[1,128,1120]{1,2,0:T(8,128)(2,1)S(1)} %bitcast.13) | data formatting | bytes 573440
  49.7 0.3 copy-done
  50.0 0.7 %copy.15 = bf16[1,128,1120]{1,2,0:T(8,128)(2,1)} copy(bf16[1,128,1120]{1,2,0:T(8,128)(2,1)S(1)} %bitcast.12) | data formatting | bytes 573440
Async XLA Ops:
  46.1 1.7 %copy-start.2 = (bf16[1,1120,128]{2,1,0:T(8,128)(2,1)S(1)}, bf16[1,1120,128]{2,1,0:T(8,128)(2,1)}, u32[]{:S(2)}) copy-start(bf16[1,1120,128]{2,1,0:T(8,128)(2,1)} %get-tuple-element.9) | copy-start | bytes 860164
  47.9 1.1 %copy-start.1 = (bf16[1,1120,128]{2,1,0:T(8,128)(2,1)S(1)}, bf16[1,1120,128]{2,1,0:T(8,128)(2,1)}, u32[]{:S(2)}) copy-start(bf16[1,1120,128]{2,1,0:T(8,128)(2,1)} %get-tuple-element.10) | copy-start | bytes 860164
  48.9 1.1 %copy-start = (bf16[1,1120,128]{2,1,0:T(8,128)(2,1)S(1)}, bf16[1,1120,128]{2,1,0:T(8,128)(2,1)}, u32[]{:S(2)}) copy-start(bf16[1,1120,128]{2,1,0:T(8,128)(2,1)} %get-tuple-element.11) | copy-start | bytes 860164

commit v3 on v2

--- a/solution.py
+++ b/solution.py
@@ -11,6 +11,7 @@
 LANES = 128
 SUBLANES = 8
 CHUNKS = 2
+VMEM_LIMIT = 24 * 1024 * 1024
 MESH = pl.DeviceIdType.MESH
 
 
@@ -47,20 +48,31 @@
     n_space, n_tm, chunks, piece,
     q_ref, k_ref, v_ref, g_ref,
     mixed_ref, gq_ref, gk_ref, gv_ref,
-    local, incoming, reduced, earlier, running, whole,
-    rs_send, rs_recv, tm_send, tm_recv, ag_send, ag_recv,
+    local, partner_half, half, incoming, reduced, earlier, running, whole,
+    pair_send, pair_recv, rs_send, rs_recv, tm_send, tm_recv,
+    ag_send, ag_recv, relay_send, relay_recv,
 ):
     me = lax.axis_index("space")
     group = lax.axis_index("tm")
+    sites = n_space // 2
+    site, side = lax.div(me, 2), lax.rem(me, 2)
+    partner = me + 1 - 2 * side
+    part = sites * piece
     rows = q_ref.shape[2]
     spare = LANES - HEAD_DIM
     ids = lax.broadcasted_iota(jnp.int32, (spare, rows), 0)
 
+    def device(d):
+        return 2 * lax.rem(site + d, sites) + side
+
+    def rows_of(which, owner):
+        start = which * part + owner * piece
+        return pl.ds(pl.multiple_of(start, SUBLANES), piece)
+
     barrier = pltpu.get_barrier_semaphore()
-    for d in range(1, n_space):
-        pl.semaphore_signal(
-            barrier, inc=1, device_id={"space": lax.rem(me + d, n_space)}, device_id_type=MESH
-        )
+    pl.semaphore_signal(barrier, inc=1, device_id={"space": partner}, device_id_type=MESH)
+    for d in range(1, sites):
+        pl.semaphore_signal(barrier, inc=1, device_id={"space": device(d)}, device_id_type=MESH)
     for d in range(1, n_tm):
         pl.semaphore_signal(
             barrier, inc=1, device_id={"tm": lax.rem(group + d, n_tm)}, device_id_type=MESH
@@ -73,14 +85,25 @@
         tail = jnp.where(ids < ones, 1.0, 0.0).astype(jnp.bfloat16)
         return jnp.concatenate([v_ref[0, span(h)], tail], axis=0)
 
+    def pair_copy(phase, c):
+        start = pl.multiple_of((1 - side) * part, SUBLANES)
+        return pltpu.make_async_remote_copy(
+            src_ref=local.at[phase, c, pl.ds(start, part)],
+            dst_ref=partner_half.at[phase, c],
+            send_sem=pair_send.at[phase, c],
+            recv_sem=pair_recv.at[phase, c],
+            device_id={"space": partner},
+            device_id_type=MESH,
+        )
+
     def scatter_copy(phase, c, d):
-        peer = lax.rem(me + d, n_space)
-        return pltpu.make_async_remote_copy(
-            src_ref=local.at[phase, c, pl.ds(pl.multiple_of(peer * piece, SUBLANES), piece)],
+        owner = lax.rem(site + d, sites)
+        return pltpu.make_async_remote_copy(
+            src_ref=half.at[phase, c, pl.ds(pl.multiple_of(owner * piece, SUBLANES), piece)],
             dst_ref=incoming.at[phase, c, d - 1],
             send_sem=rs_send.at[phase, c, d - 1],
             recv_sem=rs_recv.at[phase, c, d - 1],
-            device_id={"space": peer},
+            device_id={"space": device(d)},
             device_id_type=MESH,
         )
 
@@ -97,13 +120,23 @@
         )
 
     def gather_copy(phase, c, d):
-        peer = lax.rem(me + d, n_space)
         return pltpu.make_async_remote_copy(
             src_ref=running.at[phase, c],
-            dst_ref=whole.at[phase, c, pl.ds(pl.multiple_of(me * piece, SUBLANES), piece)],
+            dst_ref=whole.at[phase, c, rows_of(side, site)],
             send_sem=ag_send.at[phase, c, d - 1],
             recv_sem=ag_recv.at[phase, c, d - 1],
-            device_id={"space": peer},
+            device_id={"space": device(d)},
+            device_id_type=MESH,
+        )
+
+    def relay_copy(phase, c, d):
+        rows = rows_of(side, lax.rem(site + sites - d, sites))
+        return pltpu.make_async_remote_copy(
+            src_ref=running.at[phase, c] if d == 0 else whole.at[phase, c, rows],
+            dst_ref=whole.at[phase, c, rows],
+            send_sem=relay_send.at[phase, c, d],
+            recv_sem=relay_recv.at[phase, c, d],
+            device_id={"space": partner},
             device_id_type=MESH,
         )
 
@@ -113,13 +146,19 @@
     def hears_from(phase, d):
         return group - d >= 0 if phase == 0 else group + d < n_tm
 
+    def exchange(phase, c):
+        pair_copy(phase, c).start()
+
     def scatter(phase, c):
-        for d in range(1, n_space):
+        pair_copy(phase, c).wait_recv()
+        start = pl.multiple_of(side * part, SUBLANES)
+        half[phase, c] = local[phase, c, pl.ds(start, part)] + partner_half[phase, c]
+        for d in range(1, sites):
             scatter_copy(phase, c, d).start()
 
     def reduce(phase, c):
-        total = local[phase, c, pl.ds(pl.multiple_of(me * piece, SUBLANES), piece)]
-        for d in range(1, n_space):
+        total = half[phase, c, pl.ds(pl.multiple_of(site * piece, SUBLANES), piece)]
+        for d in range(1, sites):
             scatter_copy(phase, c, d).wait_recv()
             total = total + incoming[phase, c, d - 1]
         reduced[phase, c] = total
@@ -135,13 +174,19 @@
             def _():
                 group_copy(phase, c, d).wait_recv()
                 running[phase, c] = running[phase, c] + earlier[phase, c, d - 1]
-        for d in range(1, n_space):
+        for d in range(1, sites):
             gather_copy(phase, c, d).start()
-        whole[phase, c, pl.ds(pl.multiple_of(me * piece, SUBLANES), piece)] = running[phase, c]
+        relay_copy(phase, c, 0).start()
+        whole[phase, c, rows_of(side, site)] = running[phase, c]
+
+    def relay(phase, c):
+        for d in range(1, sites):
+            gather_copy(phase, c, d).wait_recv()
+            relay_copy(phase, c, d).start()
 
     def arrive(phase, c):
-        for d in range(1, n_space):
-            gather_copy(phase, c, d).wait_recv()
+        for d in range(sites):
+            relay_copy(phase, c, d).wait_recv()
 
     def pad(phase, c, size):
         spare_rows = n_space * piece - size * HEAD_DIM
@@ -216,32 +261,46 @@
     for c in range(count):
         states(c)
         if c == 0:
-            pl.semaphore_wait(barrier, n_space - 1 + n_tm - 1)
-        scatter(0, c)
-    for c in range(count):
-        reduce(0, c)
-    for c in range(count):
-        gather(0, c)
-    for c in range(count):
-        arrive(0, c)
-        queries(c)
-        scatter(1, c)
-    for c in range(count):
-        reduce(1, c)
-    for c in range(count):
-        gather(1, c)
-    for c in range(count):
-        arrive(1, c)
-        keys(c)
+            pl.semaphore_wait(barrier, 1 + sites - 1 + n_tm - 1)
+        exchange(0, c)
+    for phase, last in ((0, queries), (1, keys)):
+        for c in range(count):
+            scatter(phase, c)
+        for c in range(count):
+            reduce(phase, c)
+        for c in range(count):
+            gather(phase, c)
+        for c in range(count):
+            relay(phase, c)
+        for c in range(count):
+            arrive(phase, c)
+            last(c)
+            if phase == 0:
+                exchange(1, c)
     for phase in range(2):
         for c in range(count):
-            for d in range(1, n_space):
+            pair_copy(phase, c).wait_send()
+            for d in range(1, sites):
                 scatter_copy(phase, c, d).wait_send()
                 gather_copy(phase, c, d).wait_send()
+            for d in range(sites):
+                relay_copy(phase, c, d).wait_send()
             for d in range(1, n_tm):
                 @pl.when(sends_to(phase, d))
                 def _():
                     group_copy(phase, c, d).wait_send()
+
+
+def store(*refs):
+    sources, targets, sems = refs[:4], refs[4:8], refs[8]
+    copies = [
+        pltpu.make_async_copy(source, target, sems.at[i])
+        for i, (source, target) in enumerate(zip(sources, targets))
+    ]
+    for copy in copies:
+        copy.start()
+    for copy in copies:
+        copy.wait()
 
 
 def solution(mesh):
@@ -258,28 +317,46 @@
         vmem = pl.BlockSpec(memory_space=pltpu.VMEM)
         f32 = jnp.float32
         dma = pltpu.SemaphoreType.DMA
-        peers, others = max(n_space - 1, 1), max(n_tm - 1, 1)
+        sites, others = n_space // 2, max(n_tm - 1, 1)
+        peers = max(sites - 1, 1)
         outs = pl.pallas_call(
             functools.partial(kernel, n_space, n_tm, chunks, piece),
-            out_shape=[jax.ShapeDtypeStruct(args[0].shape, jnp.bfloat16)] * 4,
+            out_shape=[pltpu.VMEM(args[0].shape, jnp.bfloat16)] * 4,
             in_specs=[vmem] * 4,
             out_specs=[vmem] * 4,
             scratch_shapes=[
                 pltpu.VMEM((2, count, n_space * piece, LANES), f32),
+                pltpu.VMEM((2, count, sites * piece, LANES), f32),
+                pltpu.VMEM((2, count, sites * piece, LANES), f32),
                 pltpu.VMEM((2, count, peers, piece, LANES), f32),
                 pltpu.VMEM((2, count, piece, LANES), f32),
                 pltpu.VMEM((2, count, others, piece, LANES), f32),
                 pltpu.VMEM((2, count, piece, LANES), f32),
                 pltpu.VMEM((2, count, n_space * piece, LANES), f32),
+                dma((2, count)),
+                dma((2, count)),
                 dma((2, count, peers)),
                 dma((2, count, peers)),
                 dma((2, count, others)),
                 dma((2, count, others)),
                 dma((2, count, peers)),
                 dma((2, count, peers)),
+                dma((2, count, sites)),
+                dma((2, count, sites)),
             ],
-            compiler_params=pltpu.CompilerParams(collective_id=0, has_side_effects=True),
+            compiler_params=pltpu.CompilerParams(
+                collective_id=0, has_side_effects=True, vmem_limit_bytes=VMEM_LIMIT
+            ),
         )(*args)
+        anywhere = pl.BlockSpec(memory_space=pl.ANY)
+        outs = pl.pallas_call(
+            store,
+            out_shape=[jax.ShapeDtypeStruct(args[0].shape, jnp.bfloat16)] * 4,
+            in_specs=[vmem] * 4,
+            out_specs=[anywhere] * 4,
+            scratch_shapes=[dma((4,))],
+            compiler_params=pltpu.CompilerParams(vmem_limit_bytes=VMEM_LIMIT),
+        )(*outs)
         return tuple(jnp.swapaxes(out, 1, 2) for out in outs)
 
     return jax.shard_map(

time: 51 us -> 47.9 us (0.939)
  Pallas kernels: 45.5 us -> 42.9 us
  local copies, waits for them, and re-layouts: 4.57 us -> 3.83 us
    pallas_call x1, Pallas kernels: 45.5 us -> 41.9 us  [body(): pl.pallas_call(functools.partial(kernel, n_space, n_tm, chunks, piece), o...]
    pallas_call x0 -> x1, Pallas kernels: none -> 1.03 us  [body(): pl.pallas_call(store, out_shape=[jax.ShapeDtypeStruct(args[0].shape, jnp....]
    unnamed x10 -> x8, local copies, waits for them, and re-layouts: 4.57 us -> 3.83 us
where the time goes in v3:
time: 47.9 us; the launch traced here: 47.4 us
  Pallas kernels  42.9 us (90%)
  local copies, waits for them, and re-layouts  3.83 us (8%)
  between operations  0.65 us (1%)
    pallas_call x1, Pallas kernels, body(): pl.pallas_call(functools.partial(kernel, n_space, n_tm, chunks, piece), o...  41.9 us
    unnamed x8, local copies, waits for them, and re-layouts  3.83 us
    pallas_call x1, Pallas kernels, body(): pl.pallas_call(store, out_shape=[jax.ShapeDtypeStruct(args[0].shape, jnp....  1.03 us

profile of v3, /device:TPU:0, one launch (start us, length us, event | category | flops | bytes accessed | tf_op | source)
XLA Modules:
  0.0 47.4 jit_solution(8351371367488974997)
XLA Ops:
  0.6 0.0 copy-start
  0.6 0.9 %copy-done = bf16[1,128,1120]{1,2,0:T(8,128)(2,1)S(1)} copy-done((bf16[1,128,1120]{1,2,0:T(8,128)(2,1)S(1)}, bf16[1,128,1120]{1,2,0:T(8,128)(2,1)}, u32[]{:S(2)}) %copy-start) | copy-done | bytes 286744
  1.6 0.0 copy-start.1
  1.6 1.0 %copy-done.1 = bf16[1,128,1120]{1,2,0:T(8,128)(2,1)S(1)} copy-done((bf16[1,128,1120]{1,2,0:T(8,128)(2,1)S(1)}, bf16[1,128,1120]{1,2,0:T(8,128)(2,1)}, u32[]{:S(2)}) %copy-start.1) | copy-done | bytes 286744
  2.5 0.0 copy-start.2
  2.6 1.0 %copy-done.2 = bf16[1,128,1120]{1,2,0:T(8,128)(2,1)S(1)} copy-done((bf16[1,128,1120]{1,2,0:T(8,128)(2,1)S(1)}, bf16[1,128,1120]{1,2,0:T(8,128)(2,1)}, u32[]{:S(2)}) %copy-start.2) | copy-done | bytes 286744
  3.5 0.0 copy-start.3
  3.5 1.0 %copy-done.3 = bf16[1,128,1120]{1,2,0:T(8,128)(2,1)S(1)} copy-done((bf16[1,128,1120]{1,2,0:T(8,128)(2,1)S(1)}, bf16[1,128,1120]{1,2,0:T(8,128)(2,1)}, u32[]{:S(2)}) %copy-start.3) | copy-done | bytes 286744
  4.5 41.9 %shard_map.75 = (bf16[1,1120,128]{2,1,0:T(8,128)(2,1)S(1)}, bf16[1,1120,128]{2,1,0:T(8,128)(2,1)S(1)}, bf16[1,1120,128]{2,1,0:T(8,128)(2,1)S(1)}, bf16[1,1120,128]{2,1,0:T(8,128)(2,1)S(1)}) custom-call(bf16[1,1120,128]{2,1,0:T(8,128)(2,1)S(1)} %bitcast.8, bf16[1,1120,128]{2,1,0:T(8,128)(2,1)S(1)} %bitcast.9, bf16[1,1120,128]{2,1,0:T(8,128)(2,1)S(1)} %bitcast.10, ...), custom_call_target="tpu_custom_call" | custom-call | tf_op jit(solution)/shard_map/pallas_call | solution.py:322
  46.4 1.0 %shard_map.76 = (bf16[1,1120,128]{2,1,0:T(8,128)(2,1)}, bf16[1,1120,128]{2,1,0:T(8,128)(2,1)}, bf16[1,1120,128]{2,1,0:T(8,128)(2,1)}, bf16[1,1120,128]{2,1,0:T(8,128)(2,1)}) custom-call(bf16[1,1120,128]{2,1,0:T(8,128)(2,1)S(1)} %get-tuple-element.12.refs_0_, bf16[1,1120,128]{2,1,0:T(8,128)(2,1)S(1)} %get-tuple-element.13.refs_1_, ...), custom_call_target="tpu_custom_call" | custom-call | tf_op jit(solution)/shard_map/pallas_call | solution.py:352
Async XLA Ops:
  0.6 1.0 %copy-start = (bf16[1,128,1120]{1,2,0:T(8,128)(2,1)S(1)}, bf16[1,128,1120]{1,2,0:T(8,128)(2,1)}, u32[]{:S(2)}) copy-start(bf16[1,128,1120]{1,2,0:T(8,128)(2,1)} %param.4) | copy-start | bytes 860164
  1.6 1.0 %copy-start.1 = (bf16[1,128,1120]{1,2,0:T(8,128)(2,1)S(1)}, bf16[1,128,1120]{1,2,0:T(8,128)(2,1)}, u32[]{:S(2)}) copy-start(bf16[1,128,1120]{1,2,0:T(8,128)(2,1)} %param.5) | copy-start | bytes 860164
  2.5 1.0 %copy-start.2 = (bf16[1,128,1120]{1,2,0:T(8,128)(2,1)S(1)}, bf16[1,128,1120]{1,2,0:T(8,128)(2,1)}, u32[]{:S(2)}) copy-start(bf16[1,128,1120]{1,2,0:T(8,128)(2,1)} %param.6) | copy-start | bytes 860164
  3.5 1.0 %copy-start.3 = (bf16[1,128,1120]{1,2,0:T(8,128)(2,1)S(1)}, bf16[1,128,1120]{1,2,0:T(8,128)(2,1)}, u32[]{:S(2)}) copy-start(bf16[1,128,1120]{1,2,0:T(8,128)(2,1)} %param.7) | copy-start | bytes 860164

commit v4 on v3

--- a/solution.py
+++ b/solution.py
@@ -10,8 +10,11 @@
 HEAD_DIM = 112
 LANES = 128
 SUBLANES = 8
-CHUNKS = 2
+CHUNKS = 3
 VMEM_LIMIT = 24 * 1024 * 1024
+KERNEL_LIMIT = 65700000
+DUE = (0.0, 2.0, 5.0, 8.5, 11.0, 12.5, 15.0, 18.0, 21.5, 24.0, 25.5)
+SKEW = 1.2
 MESH = pl.DeviceIdType.MESH
 
 
@@ -45,19 +48,19 @@
 
 
 def kernel(
-    n_space, n_tm, chunks, piece,
+    n_space, n_tm, chunks, pieces,
+    q_hbm, k_hbm, v_hbm, g_hbm,
+    mixed_ref, gq_ref, gk_ref, gv_ref,
     q_ref, k_ref, v_ref, g_ref,
-    mixed_ref, gq_ref, gk_ref, gv_ref,
     local, partner_half, half, incoming, reduced, earlier, running, whole,
     pair_send, pair_recv, rs_send, rs_recv, tm_send, tm_recv,
-    ag_send, ag_recv, relay_send, relay_recv,
+    ag_send, ag_recv, relay_send, relay_recv, load_sem,
 ):
     me = lax.axis_index("space")
     group = lax.axis_index("tm")
     sites = n_space // 2
     site, side = lax.div(me, 2), lax.rem(me, 2)
     partner = me + 1 - 2 * side
-    part = sites * piece
     rows = q_ref.shape[2]
     spare = LANES - HEAD_DIM
     ids = lax.broadcasted_iota(jnp.int32, (spare, rows), 0)
@@ -65,9 +68,15 @@
     def device(d):
         return 2 * lax.rem(site + d, sites) + side
 
-    def rows_of(which, owner):
-        start = which * part + owner * piece
-        return pl.ds(pl.multiple_of(start, SUBLANES), piece)
+    def rows_of(c, which, owner):
+        start = (which * sites + owner) * pieces[c]
+        return pl.ds(pl.multiple_of(start, SUBLANES), pieces[c])
+
+    def first_rows(c):
+        return pl.ds(0, pieces[c])
+
+    def half_rows(c):
+        return pl.ds(0, sites * pieces[c])
 
     barrier = pltpu.get_barrier_semaphore()
     pl.semaphore_signal(barrier, inc=1, device_id={"space": partner}, device_id_type=MESH)
@@ -81,15 +90,23 @@
     def span(h):
         return pl.ds(h * HEAD_DIM, HEAD_DIM)
 
+    def load(source, target, which, c):
+        first, size = chunks[c]
+        rows_in = pl.ds(first * HEAD_DIM, size * HEAD_DIM)
+        return pltpu.make_async_copy(
+            source.at[0, rows_in], target.at[0, rows_in], load_sem.at[which, c]
+        )
+
     def value_wide(h, ones):
         tail = jnp.where(ids < ones, 1.0, 0.0).astype(jnp.bfloat16)
         return jnp.concatenate([v_ref[0, span(h)], tail], axis=0)
 
     def pair_copy(phase, c):
+        part = sites * pieces[c]
         start = pl.multiple_of((1 - side) * part, SUBLANES)
         return pltpu.make_async_remote_copy(
             src_ref=local.at[phase, c, pl.ds(start, part)],
-            dst_ref=partner_half.at[phase, c],
+            dst_ref=partner_half.at[phase, c, half_rows(c)],
             send_sem=pair_send.at[phase, c],
             recv_sem=pair_recv.at[phase, c],
             device_id={"space": partner},
@@ -99,8 +116,10 @@
     def scatter_copy(phase, c, d):
         owner = lax.rem(site + d, sites)
         return pltpu.make_async_remote_copy(
-            src_ref=half.at[phase, c, pl.ds(pl.multiple_of(owner * piece, SUBLANES), piece)],
-            dst_ref=incoming.at[phase, c, d - 1],
+            src_ref=half.at[
+                phase, c, pl.ds(pl.multiple_of(owner * pieces[c], SUBLANES), pieces[c])
+            ],
+            dst_ref=incoming.at[phase, c, d - 1, first_rows(c)],
             send_sem=rs_send.at[phase, c, d - 1],
             recv_sem=rs_recv.at[phase, c, d - 1],
             device_id={"space": device(d)},
@@ -111,8 +130,8 @@
         peer = group + d if phase == 0 else group - d
         peer = jnp.clip(peer, 0, n_tm - 1)
         return pltpu.make_async_remote_copy(
-            src_ref=reduced.at[phase, c],
-            dst_ref=earlier.at[phase, c, d - 1],
+            src_ref=reduced.at[phase, c, first_rows(c)],
+            dst_ref=earlier.at[phase, c, d - 1, first_rows(c)],
             send_sem=tm_send.at[phase, c, d - 1],
             recv_sem=tm_recv.at[phase, c, d - 1],
             device_id={"tm": peer},
@@ -121,8 +140,8 @@
 
     def gather_copy(phase, c, d):
         return pltpu.make_async_remote_copy(
-            src_ref=running.at[phase, c],
-            dst_ref=whole.at[phase, c, rows_of(side, site)],
+            src_ref=running.at[phase, c, first_rows(c)],
+            dst_ref=whole.at[phase, c, rows_of(c, side, site)],
             send_sem=ag_send.at[phase, c, d - 1],
             recv_sem=ag_recv.at[phase, c, d - 1],
             device_id={"space": device(d)},
@@ -130,9 +149,9 @@
         )
 
     def relay_copy(phase, c, d):
-        rows = rows_of(side, lax.rem(site + sites - d, sites))
+        rows = rows_of(c, side, lax.rem(site + sites - d, sites))
         return pltpu.make_async_remote_copy(
-            src_ref=running.at[phase, c] if d == 0 else whole.at[phase, c, rows],
+            src_ref=running.at[phase, c, first_rows(c)] if d == 0 else whole.at[phase, c, rows],
             dst_ref=whole.at[phase, c, rows],
             send_sem=relay_send.at[phase, c, d],
             recv_sem=relay_recv.at[phase, c, d],
@@ -151,18 +170,21 @@
 
     def scatter(phase, c):
         pair_copy(phase, c).wait_recv()
+        part = sites * pieces[c]
         start = pl.multiple_of(side * part, SUBLANES)
-        half[phase, c] = local[phase, c, pl.ds(start, part)] + partner_half[phase, c]
+        half[phase, c, half_rows(c)] = (
+            local[phase, c, pl.ds(start, part)] + partner_half[phase, c, half_rows(c)]
+        )
         for d in range(1, sites):
             scatter_copy(phase, c, d).start()
 
     def reduce(phase, c):
-        total = half[phase, c, pl.ds(pl.multiple_of(site * piece, SUBLANES), piece)]
+        total = half[phase, c, pl.ds(pl.multiple_of(site * pieces[c], SUBLANES), pieces[c])]
         for d in range(1, sites):
             scatter_copy(phase, c, d).wait_recv()
-            total = total + incoming[phase, c, d - 1]
-        reduced[phase, c] = total
-        running[phase, c] = total
+            total = total + incoming[phase, c, d - 1, first_rows(c)]
+        reduced[phase, c, first_rows(c)] = total
+        running[phase, c, first_rows(c)] = total
         for d in range(1, n_tm):
             @pl.when(sends_to(phase, d))
             def _():
@@ -173,11 +195,13 @@
             @pl.when(hears_from(phase, d))
             def _():
                 group_copy(phase, c, d).wait_recv()
-                running[phase, c] = running[phase, c] + earlier[phase, c, d - 1]
+                running[phase, c, first_rows(c)] = (
+                    running[phase, c, first_rows(c)] + earlier[phase, c, d - 1, first_rows(c)]
+                )
         for d in range(1, sites):
             gather_copy(phase, c, d).start()
         relay_copy(phase, c, 0).start()
-        whole[phase, c, rows_of(side, site)] = running[phase, c]
+        whole[phase, c, rows_of(c, side, site)] = running[phase, c, first_rows(c)]
 
     def relay(phase, c):
         for d in range(1, sites):
@@ -189,7 +213,7 @@
             relay_copy(phase, c, d).wait_recv()
 
     def pad(phase, c, size):
-        spare_rows = n_space * piece - size * HEAD_DIM
+        spare_rows = n_space * pieces[c] - size * HEAD_DIM
         if spare_rows:
             local[phase, c, pl.ds(size * HEAD_DIM, spare_rows)] = jnp.zeros(
                 (spare_rows, LANES), jnp.float32
@@ -258,25 +282,43 @@
             ).astype(jnp.bfloat16)
 
     count = len(chunks)
-    for c in range(count):
+
+    def start(c):
+        if c == 0:
+            for each in range(count):
+                load(k_hbm, k_ref, 0, each).start()
+                load(v_hbm, v_ref, 1, each).start()
+            for each in range(count):
+                load(q_hbm, q_ref, 2, each).start()
+                load(g_hbm, g_ref, 3, each).start()
+        load(k_hbm, k_ref, 0, c).wait()
+        load(v_hbm, v_ref, 1, c).wait()
         states(c)
         if c == 0:
             pl.semaphore_wait(barrier, 1 + sites - 1 + n_tm - 1)
         exchange(0, c)
-    for phase, last in ((0, queries), (1, keys)):
-        for c in range(count):
-            scatter(phase, c)
-        for c in range(count):
-            reduce(phase, c)
-        for c in range(count):
-            gather(phase, c)
-        for c in range(count):
-            relay(phase, c)
-        for c in range(count):
-            arrive(phase, c)
-            last(c)
-            if phase == 0:
-                exchange(1, c)
+
+    def middle(c):
+        arrive(0, c)
+        load(q_hbm, q_ref, 2, c).wait()
+        load(g_hbm, g_ref, 3, c).wait()
+        queries(c)
+        exchange(1, c)
+
+    def finish(c):
+        arrive(1, c)
+        keys(c)
+
+    stages = [start]
+    for phase, last in ((0, middle), (1, finish)):
+        for stage in (scatter, reduce, gather, relay):
+            stages.append(functools.partial(stage, phase))
+        stages.append(last)
+    order = sorted(
+        (DUE[s] + SKEW * c, s, c) for s in range(len(stages)) for c in range(count)
+    )
+    for _, s, c in order:
+        stages[s](c)
     for phase in range(2):
         for c in range(count):
             pair_copy(phase, c).wait_send()
@@ -311,8 +353,8 @@
         args = [jnp.swapaxes(arg, 1, 2) for arg in args]
         heads = args[0].shape[1] // HEAD_DIM
         chunks = split_heads(heads)
-        largest = max(size for _, size in chunks)
-        piece = -(-largest * HEAD_DIM // (SUBLANES * n_space)) * SUBLANES
+        pieces = [-(-size * HEAD_DIM // (SUBLANES * n_space)) * SUBLANES for _, size in chunks]
+        piece = max(pieces)
         count = len(chunks)
         vmem = pl.BlockSpec(memory_space=pltpu.VMEM)
         f32 = jnp.float32
@@ -320,11 +362,12 @@
         sites, others = n_space // 2, max(n_tm - 1, 1)
         peers = max(sites - 1, 1)
         outs = pl.pallas_call(
-            functools.partial(kernel, n_space, n_tm, chunks, piece),
+            functools.partial(kernel, n_space, n_tm, chunks, pieces),
             out_shape=[pltpu.VMEM(args[0].shape, jnp.bfloat16)] * 4,
-            in_specs=[vmem] * 4,
+            in_specs=[pl.BlockSpec(memory_space=pltpu.HBM)] * 4,
             out_specs=[vmem] * 4,
-            scratch_shapes=[
+            scratch_shapes=[pltpu.VMEM(args[0].shape, jnp.bfloat16)] * 4
+            + [
                 pltpu.VMEM((2, count, n_space * piece, LANES), f32),
                 pltpu.VMEM((2, count, sites * piece, LANES), f32),
                 pltpu.VMEM((2, count, sites * piece, LANES), f32),
@@ -343,9 +386,10 @@
                 dma((2, count, peers)),
                 dma((2, count, sites)),
                 dma((2, count, sites)),
+                dma((4, count)),
             ],
             compiler_params=pltpu.CompilerParams(
-                collective_id=0, has_side_effects=True, vmem_limit_bytes=VMEM_LIMIT
+                collective_id=0, has_side_effects=True, vmem_limit_bytes=KERNEL_LIMIT
             ),
         )(*args)
         anywhere = pl.BlockSpec(memory_space=pl.ANY)

time: 47.9 us -> 43.9 us (0.916)
  local copies, waits for them, and re-layouts: 3.83 us -> 0 us
    unnamed x8 -> x0, local copies, waits for them, and re-layouts: 3.83 us -> none
where the time goes in v4:
time: 43.9 us; the launch traced here: 43.4 us
  Pallas kernels  42.8 us (97%)
  between operations  0.64 us (1%)
    pallas_call x1, Pallas kernels, body(): pl.pallas_call(functools.partial(kernel, n_space, n_tm, chunks, pieces),...  41.8 us
    pallas_call x1, Pallas kernels, body(): pl.pallas_call(store, out_shape=[jax.ShapeDtypeStruct(args[0].shape, jnp....  1.03 us

profile of v4, /device:TPU:0, one launch (start us, length us, event | category | flops | bytes accessed | tf_op | source)
XLA Modules:
  0.0 43.4 jit_solution(212124901425631767)
XLA Ops:
  0.6 41.8 %shard_map.75 = (bf16[1,1120,128]{2,1,0:T(8,128)(2,1)S(1)}, bf16[1,1120,128]{2,1,0:T(8,128)(2,1)S(1)}, bf16[1,1120,128]{2,1,0:T(8,128)(2,1)S(1)}, bf16[1,1120,128]{2,1,0:T(8,128)(2,1)S(1)}) custom-call(bf16[1,1120,128]{2,1,0:T(8,128)(2,1)} %bitcast.8, bf16[1,1120,128]{2,1,0:T(8,128)(2,1)} %bitcast.9, bf16[1,1120,128]{2,1,0:T(8,128)(2,1)} %bitcast.10, ...), custom_call_target="tpu_custom_call" | custom-call | tf_op jit(solution)/shard_map/pallas_call | solution.py:364
  42.4 1.0 %shard_map.76 = (bf16[1,1120,128]{2,1,0:T(8,128)(2,1)}, bf16[1,1120,128]{2,1,0:T(8,128)(2,1)}, bf16[1,1120,128]{2,1,0:T(8,128)(2,1)}, bf16[1,1120,128]{2,1,0:T(8,128)(2,1)}) custom-call(bf16[1,1120,128]{2,1,0:T(8,128)(2,1)S(1)} %get-tuple-element.12.refs_0_, bf16[1,1120,128]{2,1,0:T(8,128)(2,1)S(1)} %get-tuple-element.13.refs_1_, ...), custom_call_target="tpu_custom_call" | custom-call | tf_op jit(solution)/shard_map/pallas_call | solution.py:396
